TPU v7x, 512 devices: a whole 4x8x8 slice. The times are simulated.
512 devices in a mesh: loop: 32 (over z_lo, x, core), grp: 16 (over z_hi, y).
Axes of the slice: x: 4, y: 8, z: 8 (z_hi: 2, z_lo: 4; z = z_hi * 4 + z_lo), core: 2. Of those that a mesh axis runs over, the one named last changes fastest.
Arguments:
- queries: bfloat16 [131072, 512], P(('loop', 'grp')), may hold values from -24 to 24
- key_rows: bfloat16 [131072, 512], P(('loop', 'grp')), may hold values from -4 to 4
- value_rows: bfloat16 [131072, 512], P(('loop', 'grp')), may hold values from -6 to 6
- out_weight: bfloat16 [512, 512], replicated, may hold values from -0.25 to 0.25
- tile_list: int32 [512, 4], P(('loop', 'grp')), may hold values from 0 to 7, as said below
- expander_order: int32 [3, 131072], P(None, ('loop', 'grp')), may hold values from 0 to 255, as said below
- expander_bias: float32 [3, 8], replicated, may hold values from 2 to 6
Outputs:
- layer_output: bfloat16 [131072, 512], P(('loop', 'grp'))
Inputs may be any that keep to these rules, and one draw needn't show every extreme that they name: `tile_list`: entry 0 of every row is 3, the partition's own block. Each other entry is 3 + o for a loop offset o with 0 < |o| <= 3, distinct within a row, or the padding value 2 * 3 + 1; every row has at least one non-padding neighbour entry. `expander_order`: for each matching and each partition, the 256 entries of that partition are a permutation of 0 to 255.
All inputs are finite; a program needn't handle non-finite values.
Results may differ from a plain program's by a relative error of at most 0.0075.
Values may be sent and summed in bfloat16 or wider, within the bound.
A program may use at most 128 MiB of HBM per device.

v0:
```python
import jax
import jax.numpy as jnp
from jax import lax
from jax.sharding import PartitionSpec as P

HEADS = 8
RADIUS = 3
MATCHINGS = 3


NEG_FILL = -1e30


def passed_along(array, axis, by):
    peers = lax.axis_size(axis)
    return lax.ppermute(array, axis, [(i, (i + by) % peers) for i in range(peers)])


def absorb(running, query_here, kv_block, key_mask):
    run_max, run_sum, run_acc = running
    piece_rows = kv_block.shape[0]
    model_width = kv_block.shape[1] // 2
    head_count = query_here.shape[1]
    block_keys = kv_block[:, :model_width].reshape(piece_rows, head_count, -1)
    block_vals = kv_block[:, model_width:].reshape(piece_rows, head_count, -1)
    score_scale = query_here.shape[2] ** (-0.5)
    scores = (
        jnp.einsum("rhe,nhe->hrn", query_here, block_keys, preferred_element_type=jnp.float32)
        * score_scale
    )
    masked = jnp.where(key_mask[None, None, :], scores, NEG_FILL)
    new_max = jnp.maximum(run_max, jnp.max(masked, axis=-1).T)
    rescale = jnp.exp(run_max - new_max)
    weights = jnp.where(key_mask[None, None, :], jnp.exp(masked - new_max.T[:, :, None]), 0.0)
    new_sum = run_sum * rescale + jnp.sum(weights, axis=-1).T
    new_acc = run_acc * rescale[:, :, None] + jnp.einsum(
        "hrn,nhe->rhe", weights.astype(jnp.bfloat16), block_vals, preferred_element_type=jnp.float32
    )
    return (new_max, new_sum, new_acc)


def absorb_live(running, query_here, kv_block, key_mask):

    def taken(state):
        return absorb(state, query_here, kv_block, key_mask)

    def skipped(state):
        return state

    return lax.cond(jnp.any(key_mask), taken, skipped, running)


def shards(queries, key_rows, value_rows, out_weight, tile_list, expander_order, expander_bias):
    row_count = queries.shape[0]
    model_width = queries.shape[1]
    head_width = model_width // HEADS
    query_here = queries.reshape(row_count, HEADS, head_width)
    paired = jnp.concatenate([key_rows, value_rows], axis=1)
    tiles_here = tile_list[0]
    initial = (
        jnp.full((row_count, HEADS), NEG_FILL, jnp.float32),
        jnp.zeros((row_count, HEADS), jnp.float32),
        jnp.zeros((row_count, HEADS, head_width), jnp.float32),
    )

    def wanted(offset):
        return jnp.full((row_count,), jnp.any(tiles_here == offset + RADIUS))

    running = absorb(initial, query_here, paired, wanted(0))
    forward_block = paired
    backward_block = paired
    for distance in range(1, RADIUS + 1):
        forward_block = passed_along(forward_block, "loop", 1)
        running = absorb_live(running, query_here, forward_block, wanted(-distance))
    for distance in range(1, RADIUS + 1):
        backward_block = passed_along(backward_block, "loop", -1)
        running = absorb_live(running, query_here, backward_block, wanted(distance))
    grp_pos = lax.axis_index("grp")
    grp_count = lax.axis_size("grp")
    bucket_size = row_count // grp_count
    ordered = paired[expander_order]
    buckets = ordered.reshape(MATCHINGS, grp_count, bucket_size, 2 * model_width)
    slot_map = jnp.bitwise_xor(grp_pos, jnp.arange(grp_count, dtype=jnp.int32))
    outgoing = jnp.take(buckets, slot_map, axis=1)
    incoming = lax.all_to_all(outgoing, "grp", split_axis=1, concat_axis=1, tiled=True)
    bucketed = jnp.take(incoming, slot_map, axis=1)
    own_bucket = bucketed[:, 0].reshape(MATCHINGS, bucket_size // 2, 2, 2 * model_width)[:, :, ::-1]
    own_bucket = own_bucket.reshape(MATCHINGS, 1, bucket_size, 2 * model_width)
    bucketed = jnp.concatenate([own_bucket, bucketed[:, 1:]], axis=1)
    flat_rows = bucketed.reshape(MATCHINGS, row_count, 2 * model_width)
    inverse = jnp.argsort(expander_order, axis=1)
    partner_kv = jnp.take_along_axis(flat_rows, inverse[:, :, None], axis=1)
    partner_keys = partner_kv[:, :, :model_width].reshape(MATCHINGS, row_count, HEADS, head_width)
    partner_vals = partner_kv[:, :, model_width:].reshape(MATCHINGS, row_count, HEADS, head_width)
    expander_scores = jnp.einsum(
        "rhe,jrhe->jrh", query_here, partner_keys, preferred_element_type=jnp.float32
    ) * head_width ** (-0.5)
    expander_scores = expander_scores + expander_bias[:, None, :]
    run_max, run_sum, run_acc = running
    final_max = jnp.maximum(run_max, jnp.max(expander_scores, axis=0))
    rescale = jnp.exp(run_max - final_max)
    expander_w = jnp.exp(expander_scores - final_max[None])
    denominator = run_sum * rescale + jnp.sum(expander_w, axis=0)
    numerator = run_acc * rescale[:, :, None] + jnp.einsum(
        "jrh,jrhe->rhe",
        expander_w.astype(jnp.bfloat16),
        partner_vals,
        preferred_element_type=jnp.float32,
    )
    attended = (
        (numerator / denominator[:, :, None]).reshape(row_count, model_width).astype(jnp.bfloat16)
    )
    return jnp.dot(attended, out_weight, preferred_element_type=jnp.float32).astype(jnp.bfloat16)


def solution(mesh):
    placed = (
        P(("loop", "grp"), None),
        P(("loop", "grp"), None),
        P(("loop", "grp"), None),
        P(),
        P(("loop", "grp"), None),
        P(None, ("loop", "grp")),
        P(),
    )
    return jax.shard_map(
        shards, mesh=mesh, in_specs=placed, out_specs=P(("loop", "grp"), None), check_vma=False
    )
```

profile of v0, /device:TPU:32, one launch (start us, length us, event | category | flops | bytes accessed | tf_op | source)
XLA Modules:
  0.0 150.2 jit_solution(16837027401801456095)
XLA Ops:
  6.6 1.0 constant_dynamic-update-slice_fusion.1
  7.6 0.7 compare_select_fusion
  8.3 1.0 constant_dynamic-update-slice_fusion
  9.3 3.6 %gather_fusion = bf16[768,1024]{1,0:T(8,128)(2,1)} fusion(bf16[256,1024]{1,0:T(8,128)(2,1)S(1)} %constant_dynamic-update-slice_fusion, s32[1024]{0:T(1024)S(1)} %get-tuple-element.352), kind=kCustom, calls=%fused_computation.2 | custom fusion | bytes 3148800 | tf_op jit(solution)/shard_map/gather | solution.py:81
  12.9 2.1 %gather_fusion.2 = bf16[16,3,16,1024]{3,2,1,0:T(8,128)(2,1)S(1)} fusion(bf16[3,16,16,1024]{3,2,1,0:T(8,128)(2,1)} %bitcast.151, s32[1024]{0:T(1024)S(1)} %get-tuple-element.351), kind=kCustom, calls=%fused_computation.clone | custom fusion | bytes 3145792 | tf_op jit(solution)/shard_map/jit(_take)/gather | solution.py:84
  14.9 1.4 select_bitcast_fusion.1
  16.3 15.8 %all-to-all-start = ((bf16[3,16,16,1024]{3,2,0,1:T(8,128)(2,1)}), bf16[3,16,16,1024]{3,2,0,1:T(8,128)(2,1)}, u32[]{:S(2)}, u32[]{:S(2)}) async-start(bf16[3,16,16,1024]{3,2,0,1:T(8,128)(2,1)} %select_bitcast_fusion.1), calls=%async_computation | async-start | bytes 3145728 | tf_op jit(solution)/shard_map/all_to_all | solution.py:85
  32.1 1.9 %collective-permute-start = (bf16[256,1024]{1,0:T(8,128)(2,1)S(1)}, bf16[256,1024]{1,0:T(8,128)(2,1)}, u32[]{:S(2)}, u32[]{:S(2)}) collective-permute-start(bf16[256,1024]{1,0:T(8,128)(2,1)S(1)} %constant_dynamic-update-slice_fusion), channel_id=1, source_target_pairs={{0,16},{16,32},{32,48},{48,64},{64,80},{80,96},{96,112},{112,128},... | collective-permute-start | bytes 1572872 | tf_op jit(solution)/shard_map/ppermute | solution.py:16
  34.1 7.6 %collective-permute-start.3 = (bf16[256,1024]{1,0:T(8,128)(2,1)S(1)}, bf16[256,1024]{1,0:T(8,128)(2,1)}, u32[]{:S(2)}, u32[]{:S(2)}) collective-permute-start(bf16[256,1024]{1,0:T(8,128)(2,1)S(1)} %constant_dynamic-update-slice_fusion), channel_id=1, source_target_pairs={{0,496},{16,0},{32,16},{48,32},{64,48},{80,64},{96,80},{112,96},{1... | collective-permute-start | bytes 1572872 | tf_op jit(solution)/shard_map/ppermute | solution.py:16
  41.6 0.6 iota.10
  42.2 0.8 compare_reduce_fusion
  43.0 0.8 copy.54
  44.0 2.1 %fusion.72 = (f32[8,256]{1,0:T(8,128)S(1)}, f32[8,256,256]{1,2,0:T(8,128)S(1)}) fusion(pred[]{:T(512)} %get-tuple-element.296, bf16[256,8,64]{0,2,1:T(8,128)(2,1)S(1)} %bitcast.143, bf16[256,8,64]{0,2,1:T(8,128)(2,1)} %bitcast.153), kind=kOutput, calls=%fused_computation.108 | convolution fusion | flops 68679680 | bytes 2629633 | tf_op jit(solution)/shard_map/rhe,nhe->hrn/dot_general | solution.py:28
  46.2 34.7 %collective-permute-done = bf16[256,1024]{1,0:T(8,128)(2,1)} collective-permute-done((bf16[256,1024]{1,0:T(8,128)(2,1)S(1)}, bf16[256,1024]{1,0:T(8,128)(2,1)}, u32[]{:S(2)}, u32[]{:S(2)}) %collective-permute-start) | collective-permute-done | bytes 524320 | tf_op jit(solution)/shard_map/ppermute | solution.py:16
  80.9 1.9 %collective-permute-start.1 = (bf16[256,1024]{1,0:T(8,128)(2,1)}, bf16[256,1024]{1,0:T(8,128)(2,1)}, u32[]{:S(2)}, u32[]{:S(2)}) collective-permute-start(bf16[256,1024]{1,0:T(8,128)(2,1)} %collective-permute-done), channel_id=1, source_target_pairs={{0,16},{16,32},{32,48},{48,64},{64,80},{80,96},{96,112},{112,128},... | collective-permute-start | bytes 1572872 | tf_op jit(solution)/shard_map/ppermute | solution.py:16
  82.8 7.6 %collective-permute-start.4 = (bf16[256,1024]{1,0:T(8,128)(2,1)}, bf16[256,1024]{1,0:T(8,128)(2,1)}, u32[]{:S(2)}, u32[]{:S(2)}) collective-permute-start(bf16[256,1024]{1,0:T(8,128)(2,1)} %collective-permute-done.3), channel_id=1, source_target_pairs={{0,496},{16,0},{32,16},{48,32},{64,48},{80,64},{96,80},{112,96},{1... | collective-permute-start | bytes 1572872 | tf_op jit(solution)/shard_map/ppermute | solution.py:16
  90.4 1.2 fusion.74
  91.5 1.1 copy.55
  92.6 2.0 %fusion.75 = f32[256,8,64]{0,2,1:T(8,128)} fusion(bf16[256,8,64]{0,2,1:T(8,128)(2,1)S(1)} %bitcast.161, f32[8,256,256]{1,2,0:T(8,128)S(1)} %get-tuple-element.350, f32[8,256]{1,0:T(8,128)S(1)} %get-tuple-element.347, pred[]{:T(512)} %get-tuple-element.296, f32[256,8]{0,1:T(8,128)S(1)} %get-tuple-element.345), kind=kOutput, calls=%fused_computation.118 | convolution fusion | flops 69861376 | bytes 2899969 | tf_op jit(solution)/shard_map/hrn,nhe->rhe/dot_general | solution.py:36
  94.7 0.9 collective-permute-done.1
  95.6 1.9 %collective-permute-start.2 = (bf16[256,1024]{1,0:T(8,128)(2,1)}, bf16[256,1024]{1,0:T(8,128)(2,1)S(1)}, u32[]{:S(2)}, u32[]{:S(2)}) collective-permute-start(bf16[256,1024]{1,0:T(8,128)(2,1)} %collective-permute-done.1), channel_id=1, source_target_pairs={{0,16},{16,32},{32,48},{48,64},{64,80},{80,96},{96,112},{112,128},... | collective-permute-start | bytes 1572872 | tf_op jit(solution)/shard_map/ppermute | solution.py:16
  97.5 7.6 %collective-permute-start.5 = (bf16[256,1024]{1,0:T(8,128)(2,1)}, bf16[256,1024]{1,0:T(8,128)(2,1)S(1)}, u32[]{:S(2)}, u32[]{:S(2)}) collective-permute-start(bf16[256,1024]{1,0:T(8,128)(2,1)} %collective-permute-done.4), channel_id=1, source_target_pairs={{0,496},{16,0},{32,16},{48,32},{64,48},{80,64},{96,80},{112,96},{1... | collective-permute-start | bytes 1572872 | tf_op jit(solution)/shard_map/ppermute | solution.py:16
  108.7 0.7 bitcast_or_fusion
  109.4 0.7 compare_and_fusion
  110.1 5.7 %conditional.6 = ((f32[256,8]{0,1:T(8,128)S(1)}, f32[256,8]{0,1:T(8,128)S(1)}, f32[256,8,64]{0,2,1:T(8,128)})) conditional(s32[]{:T(128)} %convert_element_type.56, (f32[256,8]{0,1:T(8,128)S(1)}, f32[256,8]{0,1:T(8,128)S(1)}, f32[256,8,64]{0,2,1:T(8,128)}) %tuple.43, (pred[]{:T(512)}, bf16[256,1024]{1,0:T(8,128)(2,1)}, ...), branch_computations={%region_9.10_spmd, %region_10.13_spmd} | conditional | flops 141299712 | bytes 14549083 | solution.py:50
  110.1 1.2 copy.57
  111.4 1.2 fusion
  112.6 1.1 fusion.2
  113.8 1.2 fusion.3
  115.0 0.8 copy-done.3
  115.8 5.5 %conditional.7 = ((f32[256,8]{0,1:T(8,128)S(1)}, f32[256,8]{0,1:T(8,128)S(1)}, f32[256,8,64]{0,2,1:T(8,128)})) conditional(s32[]{:T(128)} %convert_element_type.55, (f32[256,8]{0,1:T(8,128)S(1)}, f32[256,8]{0,1:T(8,128)S(1)}, f32[256,8,64]{0,2,1:T(8,128)}) %get-tuple-element.391, (pred[]{:T(512)}, bf16[256,1024]{1,0:T(8,128)(2,1)}, ...), branch_computations={%region_13.0_spmd, %region_14.17_spmd} | conditional | flops 141299712 | bytes 14549083 | solution.py:50
  115.8 1.2 copy.58
  117.1 1.1 fusion.12
  118.3 1.1 fusion.14
  119.4 1.2 fusion.15
  120.6 0.8 copy-done.5
  121.4 4.5 %conditional.11 = ((f32[256,8]{0,1:T(8,128)S(1)}, f32[256,8]{0,1:T(8,128)S(1)}, f32[256,8,64]{0,2,1:T(8,128)})) conditional(s32[]{:T(128)} %convert_element_type.51, (f32[256,8]{0,1:T(8,128)S(1)}, f32[256,8]{0,1:T(8,128)S(1)}, f32[256,8,64]{0,2,1:T(8,128)}) %get-tuple-element.395, (pred[]{:T(512)}, bf16[256,1024]{1,0:T(8,128)(2,1)S(1)}, ...), branch_computations={%region_29.30_spmd, %region_30.33_spmd} | conditional | flops 141299712 | bytes 14549083 | solution.py:50
  121.7 1.1 fusion.60
  122.8 1.1 fusion.62
  123.9 1.2 fusion.63
  125.1 0.8 copy-done.13
  125.9 2.1 %gather_fusion.3 = bf16[16,3,16,1024]{3,2,1,0:T(8,128)(2,1)S(1)} fusion(bf16[3,16,16,1024]{3,2,0,1:T(8,128)(2,1)} %all-to-all-done, s32[1024]{0:T(1024)S(1)} %get-tuple-element.351), kind=kCustom, calls=%fused_computation.1.clone | custom fusion | bytes 3145792 | tf_op jit(solution)/shard_map/jit(_take)/gather | solution.py:86
  128.0 0.2 select_bitcast_fusion
  128.4 0.7 rev.3
  129.4 9.8 %gather_fusion.1 = bf16[768,1024]{1,0:T(8,128)(2,1)} fusion(bf16[3,256,1024]{2,1,0:T(8,128)(2,1)S(1)} %bitcast.142, s32[768]{0:T(1024)S(1)} %reshape.139), kind=kCustom, calls=%fused_computation.3 | custom fusion | bytes 3151872 | tf_op jit(solution)/shard_map/jit(take_along_axis)/gather | solution.py:92
  139.2 1.7 %copy.64 = bf16[3,256,1024]{1,2,0:T(8,128)(2,1)S(1)} copy(bf16[3,256,1024]{2,1,0:T(8,128)(2,1)} %bitcast.150) | data formatting | bytes 3145728 | tf_op jit(solution)/shard_map/jit(take_along_axis)/gather | solution.py:92
  141.4 0.3 copy-done.16
  142.3 1.0 convolution_convert_fusion
  (68 shorter events, 2.2 us)
Async XLA Ops:
  6.5 135.8 %copy-start = (bf16[512,512]{1,0:T(8,128)(2,1)S(1)}, bf16[512,512]{1,0:T(8,128)(2,1)}, u32[]{:S(2)}) copy-start(bf16[512,512]{1,0:T(8,128)(2,1)} %param.24) | copy-start | bytes 1572868
  16.3 26.0 %copy-start.17 = (s32[1,4]{1,0:T(1,128)S(1)}, s32[1,4]{1,0:T(1,128)}, u32[]{:S(2)}) copy-start(s32[1,4]{1,0:T(1,128)} %param.25) | copy-start | bytes 52
  16.3 26.7 %copy-start.1 = (bf16[256,512]{1,0:T(8,128)(2,1)S(1)}, bf16[256,512]{1,0:T(8,128)(2,1)}, u32[]{:S(2)}) copy-start(bf16[256,512]{1,0:T(8,128)(2,1)} %param.22) | copy-start | bytes 786436
  16.3 27.6 %copy-start.15 = (bf16[256,512]{1,0:T(8,128)(2,1)S(1)}, bf16[256,512]{1,0:T(8,128)(2,1)}, u32[]{:S(2)}) copy-start(bf16[256,512]{1,0:T(8,128)(2,1)} %param.21) | copy-start | bytes 786436
  16.3 109.6 %all-to-all-start = ((bf16[3,16,16,1024]{3,2,0,1:T(8,128)(2,1)}), bf16[3,16,16,1024]{3,2,0,1:T(8,128)(2,1)}, u32[]{:S(2)}, u32[]{:S(2)}) async-start(bf16[3,16,16,1024]{3,2,0,1:T(8,128)(2,1)} %select_bitcast_fusion.1), calls=%async_computation | async-start | bytes 3145728 | tf_op jit(solution)/shard_map/all_to_all | solution.py:85
  32.1 76.7 %sort.19.cloned.1.call-start = ((), (), s32[]{:S(2)}) async-start(), calls=%async_computation.1 | async-start | bytes 24608 | tf_op jit(solution)/shard_map/jit(argsort)/sort | solution.py:91
  32.1 48.7 %collective-permute-start = (bf16[256,1024]{1,0:T(8,128)(2,1)S(1)}, bf16[256,1024]{1,0:T(8,128)(2,1)}, u32[]{:S(2)}, u32[]{:S(2)}) collective-permute-start(bf16[256,1024]{1,0:T(8,128)(2,1)S(1)} %constant_dynamic-update-slice_fusion), channel_id=1, source_target_pairs={{0,16},{16,32},{32,48},{48,64},{64,80},{80,96},{96,112},{112,128},... | collective-permute-start | bytes 1572872 | tf_op jit(solution)/shard_map/ppermute | solution.py:16
  34.1 48.7 %collective-permute-start.3 = (bf16[256,1024]{1,0:T(8,128)(2,1)S(1)}, bf16[256,1024]{1,0:T(8,128)(2,1)}, u32[]{:S(2)}, u32[]{:S(2)}) collective-permute-start(bf16[256,1024]{1,0:T(8,128)(2,1)S(1)} %constant_dynamic-update-slice_fusion), channel_id=1, source_target_pairs={{0,496},{16,0},{32,16},{48,32},{64,48},{80,64},{96,80},{112,96},{1... | collective-permute-start | bytes 1572872 | tf_op jit(solution)/shard_map/ppermute | solution.py:16
  80.9 14.7 %collective-permute-start.1 = (bf16[256,1024]{1,0:T(8,128)(2,1)}, bf16[256,1024]{1,0:T(8,128)(2,1)}, u32[]{:S(2)}, u32[]{:S(2)}) collective-permute-start(bf16[256,1024]{1,0:T(8,128)(2,1)} %collective-permute-done), channel_id=1, source_target_pairs={{0,16},{16,32},{32,48},{48,64},{64,80},{80,96},{96,112},{112,128},... | collective-permute-start | bytes 1572872 | tf_op jit(solution)/shard_map/ppermute | solution.py:16
  82.8 14.7 %collective-permute-start.4 = (bf16[256,1024]{1,0:T(8,128)(2,1)}, bf16[256,1024]{1,0:T(8,128)(2,1)}, u32[]{:S(2)}, u32[]{:S(2)}) collective-permute-start(bf16[256,1024]{1,0:T(8,128)(2,1)} %collective-permute-done.3), channel_id=1, source_target_pairs={{0,496},{16,0},{32,16},{48,32},{64,48},{80,64},{96,80},{112,96},{1... | collective-permute-start | bytes 1572872 | tf_op jit(solution)/shard_map/ppermute | solution.py:16
  95.6 25.8 %collective-permute-start.2 = (bf16[256,1024]{1,0:T(8,128)(2,1)}, bf16[256,1024]{1,0:T(8,128)(2,1)S(1)}, u32[]{:S(2)}, u32[]{:S(2)}) collective-permute-start(bf16[256,1024]{1,0:T(8,128)(2,1)} %collective-permute-done.1), channel_id=1, source_target_pairs={{0,16},{16,32},{32,48},{48,64},{64,80},{80,96},{96,112},{112,128},... | collective-permute-start | bytes 1572872 | tf_op jit(solution)/shard_map/ppermute | solution.py:16
  97.5 23.9 %collective-permute-start.5 = (bf16[256,1024]{1,0:T(8,128)(2,1)}, bf16[256,1024]{1,0:T(8,128)(2,1)S(1)}, u32[]{:S(2)}, u32[]{:S(2)}) collective-permute-start(bf16[256,1024]{1,0:T(8,128)(2,1)} %collective-permute-done.4), channel_id=1, source_target_pairs={{0,496},{16,0},{32,16},{48,32},{64,48},{80,64},{96,80},{112,96},{1... | collective-permute-start | bytes 1572872 | tf_op jit(solution)/shard_map/ppermute | solution.py:16
  111.4 2.4 %copy-start.2 = (f32[256,8,64]{0,2,1:T(8,128)S(1)}, f32[256,8,64]{0,2,1:T(8,128)}, u32[]{:S(2)}) copy-start(f32[256,8,64]{0,2,1:T(8,128)} %get-tuple-element.119) | copy-start | bytes 1572868 | tf_op jit(solution)/shard_map/cond
  115.0 0.8 copy-start.3
  117.1 2.2 %copy-start.4 = (f32[256,8,64]{0,2,1:T(8,128)S(1)}, f32[256,8,64]{0,2,1:T(8,128)}, u32[]{:S(2)}) copy-start(f32[256,8,64]{0,2,1:T(8,128)} %get-tuple-element.125) | copy-start | bytes 1572868 | tf_op jit(solution)/shard_map/cond
  120.6 0.8 copy-start.5
  121.7 2.2 %copy-start.12 = (f32[256,8,64]{0,2,1:T(8,128)S(1)}, f32[256,8,64]{0,2,1:T(8,128)}, u32[]{:S(2)}) copy-start(f32[256,8,64]{0,2,1:T(8,128)} %get-tuple-element.149) | copy-start | bytes 1572868 | tf_op jit(solution)/shard_map/cond
  125.1 0.8 copy-start.13
  141.1 0.7 copy-start.16
  141.2 1.0 copy-start.14
Sparse Core Ops, SparseCore 0:
  42.4 2.5 sort.21.cloned.1.call-done
  (1 shorter events, 0.0 us)
where the time goes:
time: 151 us; the launch traced here: 150 us
  starting transfers between devices  44.2 us (29%)
  waiting for transfers between devices  35.6 us (24%)
  local copies, waits for them, and re-layouts  30.7 us (20%)
  between operations  17.3 us (11%)
  matrix products  12.2 us (8%)
  other arithmetic  9.87 us (7%)
    ppermute x6, waiting for transfers between devices, passed_along(): lax.ppermute(array, axis, [(i, (i + by) % peers) for i in range(peers)])  35.6 us
    ppermute x6, starting transfers between devices, passed_along(): lax.ppermute(array, axis, [(i, (i + by) % peers) for i in range(peers)])  28.4 us
    all_to_all x1, starting transfers between devices, shards(): lax.all_to_all(outgoing, 'grp', split_axis=1, concat_axis=1, tiled=True)  15.8 us
    gather x3, local copies, waits for them, and re-layouts, shards(): partner_kv = jnp.take_along_axis(flat_rows, inverse[:, :, None], axis=1)  11.5 us
    dot_general x4, matrix products, absorb(): jnp.einsum('hrn,nhe->rhe', weights.astype(jnp.bfloat16), block_vals, pref...  5.65 us
    dot_general x4, matrix products, absorb(): jnp.einsum('rhe,nhe->hrn', query_here, block_keys, preferred_element_type...  5.55 us
    reduce_sum x4, other arithmetic, absorb(): new_sum = run_sum * rescale + jnp.sum(weights, axis=-1).T  4.43 us
    unnamed x17, local copies, waits for them, and re-layouts  3.59 us
  transfers between devices with their start and end apart: 7, of which 2 were waited for; matrix products, arithmetic and copies ran while one was open for 16% of the time, Pallas kernels for 0%

commit v1 on v0

v1 whole, which is shorter than its diff:
```python
import jax
import jax.numpy as jnp
from jax import lax
from jax.experimental import pallas as pl
from jax.experimental.pallas import tpu as pltpu
from jax.sharding import PartitionSpec as P

MESH = pl.DeviceIdType.MESH
NEG_FILL = -1e30
RADIUS = 3
BUCKET_ORDER = (15, 1, 8, 2, 14, 3, 9, 4, 13, 5, 10, 6, 12, 7, 11)


def kernel(
    sizes,
    q_hbm,
    k_hbm,
    v_hbm,
    order_hbm,
    tile_hbm,
    bias_hbm,
    att_ref,
    order_ref,
    tile_ref,
    bias_ref,
    tiles,
    q_vmem,
    q_blocks,
    send_buf,
    recv_buf,
    run_max,
    run_sum,
    run_acc,
    acc_rows,
    partner_vals,
    expander_e,
    local_sem,
    tile_send,
    tile_recv,
    exp_send,
    exp_recv,
):
    n_loop, n_grp, matchings, heads, head = sizes
    rows, width = q_vmem.shape
    bucket = rows // n_grp
    loop_pos = lax.axis_index("loop")
    grp_pos = lax.axis_index("grp")
    core = lax.rem(loop_pos, 2)

    def on_loop(by):
        return (lax.rem(loop_pos + by + n_loop, n_loop), grp_pos)

    bits = [lax.rem(grp_pos // (1 << i), 2) for i in range(n_grp.bit_length() - 1)]

    def grp_peer(b):
        peer = grp_pos
        for i, bit in enumerate(bits):
            if (b >> i) & 1:
                peer = peer + (1 - 2 * bit) * (1 << i)
        return (loop_pos, peer)

    sibling = on_loop(1 - 2 * core)
    ahead, behind = on_loop(2), on_loop(-2)
    far = on_loop(6 * core - 3)

    barrier = pltpu.get_barrier_semaphore()
    peers = [grp_peer(b) for b in BUCKET_ORDER] + [sibling, ahead, behind, far]
    for peer in peers:
        pl.semaphore_signal(barrier, inc=1, device_id=peer, device_id_type=MESH)

    loads = [
        pltpu.make_async_copy(k_hbm, tiles.at[0, 0], local_sem.at[0]),
        pltpu.make_async_copy(v_hbm, tiles.at[0, 1], local_sem.at[1]),
        pltpu.make_async_copy(order_hbm, order_ref, local_sem.at[2]),
        pltpu.make_async_copy(q_hbm, q_vmem, local_sem.at[3]),
        pltpu.make_async_copy(tile_hbm, tile_ref, local_sem.at[4]),
        pltpu.make_async_copy(bias_hbm, bias_ref, local_sem.at[5]),
    ]
    for load in loads:
        load.start()

    row_id = lax.broadcasted_iota(jnp.int32, (rows, rows), 0)

    def gather(j):
        hot = (row_id == order_ref[j : j + 1, :]).astype(jnp.float32)
        pick = jnp.transpose(hot).astype(jnp.bfloat16)
        for part in range(2):
            send_buf[j, :, part * width : (part + 1) * width] = jnp.dot(
                pick, tiles[0, part], preferred_element_type=jnp.float32
            ).astype(jnp.bfloat16)

    def exp_copy(j, b):
        where = pl.ds(b * bucket, bucket)
        return pltpu.make_async_remote_copy(
            src_ref=send_buf.at[j, where],
            dst_ref=recv_buf.at[j, where],
            send_sem=exp_send.at[j, b],
            recv_sem=exp_recv.at[j, b],
            device_id=grp_peer(b),
            device_id_type=MESH,
        )

    def tile_copy(src, slot, to):
        return pltpu.make_async_remote_copy(
            src_ref=tiles.at[src],
            dst_ref=tiles.at[slot],
            send_sem=tile_send.at[slot],
            recv_sem=tile_recv.at[slot],
            device_id=to,
            device_id_type=MESH,
        )

    to_far = tile_copy(0, 6, far)
    to_ahead = tile_copy(0, 2, ahead)
    to_behind = tile_copy(0, 3, behind)
    to_sibling = tile_copy(0, 1, sibling)
    pass_behind = tile_copy(2, 4, sibling)
    pass_ahead = tile_copy(3, 5, sibling)

    for load in loads[:3]:
        load.wait()
    gather(0)
    pl.semaphore_wait(barrier, len(peers))
    for copy in (to_ahead, to_behind, to_far, to_sibling):
        copy.start()
    for b in BUCKET_ORDER:
        exp_copy(0, b).start()
    for j in range(1, matchings):
        gather(j)
        for b in BUCKET_ORDER:
            exp_copy(j, b).start()

    for load in loads[3:]:
        load.wait()
    scale = head**-0.5
    q_scaled = q_vmem[...].astype(jnp.float32) * scale
    q_turned = jnp.transpose(q_scaled).astype(jnp.bfloat16)
    q_blocks[...] = jnp.zeros_like(q_blocks)
    for h in range(heads):
        i, half = h // 2, h % 2
        q_blocks[i, half * head : (half + 1) * head, half * rows : (half + 1) * rows] = (
            q_turned[h * head : (h + 1) * head, :]
        )
    run_max[...] = jnp.full_like(run_max, NEG_FILL)
    run_sum[...] = jnp.zeros_like(run_sum)
    run_acc[...] = jnp.zeros_like(run_acc)

    def absorb(slot, offset):
        wanted = tile_ref[0, 0] == offset + RADIUS
        for t in range(1, tile_ref.shape[1]):
            wanted = jnp.logical_or(wanted, tile_ref[0, t] == offset + RADIUS)
        fill = jnp.where(wanted, 0.0, NEG_FILL)
        v_turned = jnp.transpose(tiles[slot, 1].astype(jnp.float32)).astype(jnp.bfloat16)
        for i in range(heads // 2):
            pair = jnp.dot(
                tiles[slot, 0, :, i * 2 * head : (i + 1) * 2 * head],
                q_blocks[i],
                preferred_element_type=jnp.float32,
            )
            for half in range(2):
                h = 2 * i + half
                scores = pair[:, half * rows : (half + 1) * rows]
                old = run_max[h : h + 1, :]
                new = jnp.maximum(old, jnp.max(scores, axis=0, keepdims=True) + fill)
                weights = jnp.exp(scores - (new - fill))
                rescale = jnp.exp(old - new)
                run_max[h : h + 1, :] = new
                run_sum[h : h + 1, :] = run_sum[h : h + 1, :] * rescale + jnp.sum(
                    weights, axis=0, keepdims=True
                )
                here = slice(h * head, (h + 1) * head)
                run_acc[here, :] = run_acc[here, :] * rescale + jnp.dot(
                    v_turned[here, :],
                    weights.astype(jnp.bfloat16),
                    preferred_element_type=jnp.float32,
                )

    @pl.loop(0, 7)
    def _(slot):
        @pl.when(slot > 0)
        def _():
            tile_copy(0, slot, sibling).wait_recv()

        @pl.when(slot == 2)
        def _():
            pass_behind.start()

        @pl.when(slot == 3)
        def _():
            pass_ahead.start()

        near = 1 - 2 * core
        offset = jnp.where(
            slot < 2,
            slot * near,
            jnp.where(
                slot == 2,
                -2,
                jnp.where(
                    slot == 3,
                    2,
                    jnp.where(
                        slot == 4,
                        -1 - 2 * core,
                        jnp.where(slot == 5, 3 - 2 * core, 6 * core - 3),
                    ),
                ),
            ),
        )
        absorb(slot, offset)

    acc_rows[...] = jnp.transpose(run_acc[...])

    head_id = lax.broadcasted_iota(jnp.int32, (heads, width), 0)
    lane_id = lax.broadcasted_iota(jnp.int32, (heads, width), 1)
    in_head = jnp.logical_and(lane_id >= head_id * head, lane_id < (head_id + 1) * head)
    in_head = in_head.astype(jnp.float32).astype(jnp.bfloat16)
    bias_row = lax.broadcasted_iota(jnp.int32, (heads, rows), 0)
    lane = lax.broadcasted_iota(jnp.int32, (8, rows), 1)

    def split(x):
        high = x.astype(jnp.bfloat16)
        return high, (x - high.astype(jnp.float32)).astype(jnp.bfloat16)

    def expander(j):
        for b in BUCKET_ORDER:
            exp_copy(j, b).wait_recv()
        recv_buf[j, 0:bucket, :] = send_buf[j, 0:bucket, :]
        order = jnp.broadcast_to(order_ref[j : j + 1, :], (8, rows))
        swapped = jnp.where(
            lax.rem(lane, 2) == 0, pltpu.roll(order, rows - 1, 1), pltpu.roll(order, 1, 1)
        )
        order = jnp.where(lane < bucket, swapped, order)[0:1, :]
        back = (row_id == order).astype(jnp.float32).astype(jnp.bfloat16)
        keys = jnp.dot(back, recv_buf[j, :, :width], preferred_element_type=jnp.float32)
        partner_vals[j] = jnp.dot(
            back, recv_buf[j, :, width:], preferred_element_type=jnp.float32
        )
        terms = keys * (q_vmem[...].astype(jnp.float32) * scale)
        score = jnp.zeros((heads, rows), jnp.float32)
        for term in split(terms):
            score = score + lax.dot_general(
                in_head, term, (((1,), (1,)), ((), ())), preferred_element_type=jnp.float32
            )
        for h in range(heads):
            score = score + jnp.where(bias_row == h, bias_ref[j, h], 0.0)
        expander_e[j] = score

    for j in range(matchings):
        expander(j)

    top = run_max[...]
    for j in range(matchings):
        top = jnp.maximum(top, expander_e[j])
    block_part = jnp.exp(run_max[...] - top)
    weights = [jnp.exp(expander_e[j] - top) for j in range(matchings)]
    total = run_sum[...] * block_part
    for weight in weights:
        total = total + weight

    def spread(x):
        both = jnp.concatenate(split(x), axis=0)
        twice = jnp.concatenate([in_head, in_head], axis=0)
        return lax.dot_general(
            both, twice, (((0,), (0,)), ((), ())), preferred_element_type=jnp.float32
        )

    inverse = 1.0 / total
    attended = spread(block_part * inverse) * acc_rows[...]
    for j, weight in enumerate(weights):
        weight = weight.astype(jnp.bfloat16).astype(jnp.float32)
        attended = attended + spread(weight * inverse) * partner_vals[j]
    att_ref[...] = attended.astype(jnp.bfloat16)

    for copy in (to_ahead, to_behind, to_far, to_sibling, pass_behind, pass_ahead):
        copy.wait_send()
    for j in range(matchings):
        for b in BUCKET_ORDER:
            exp_copy(j, b).wait_send()


def solution(mesh):
    n_loop, n_grp = mesh.shape["loop"], mesh.shape["grp"]

    def shards(queries, key_rows, value_rows, out_weight, tile_list, order, bias):
        rows, width = queries.shape
        matchings, heads = bias.shape
        head = width // heads
        hbm = pl.BlockSpec(memory_space=pltpu.MemorySpace.HBM)
        vmem = pl.BlockSpec(memory_space=pltpu.VMEM)

        def body(*refs):
            kernel((n_loop, n_grp, matchings, heads, head), *refs)

        attended = pl.pallas_call(
            body,
            out_shape=jax.ShapeDtypeStruct((rows, width), jnp.bfloat16),
            in_specs=[hbm] * 6,
            out_specs=vmem,
            scratch_shapes=[
                pltpu.VMEM(order.shape, order.dtype),
                pltpu.SMEM(tile_list.shape, tile_list.dtype),
                pltpu.SMEM(bias.shape, bias.dtype),
                pltpu.VMEM((7, 2, rows, width), jnp.bfloat16),
                pltpu.VMEM((rows, width), jnp.bfloat16),
                pltpu.VMEM((heads // 2, 2 * head, 2 * rows), jnp.bfloat16),
                pltpu.VMEM((matchings, rows, 2 * width), jnp.bfloat16),
                pltpu.VMEM((matchings, rows, 2 * width), jnp.bfloat16),
                pltpu.VMEM((heads, rows), jnp.float32),
                pltpu.VMEM((heads, rows), jnp.float32),
                pltpu.VMEM((width, rows), jnp.float32),
                pltpu.VMEM((rows, width), jnp.float32),
                pltpu.VMEM((matchings, rows, width), jnp.float32),
                pltpu.VMEM((matchings, heads, rows), jnp.float32),
                pltpu.SemaphoreType.DMA((6,)),
                pltpu.SemaphoreType.DMA((7,)),
                pltpu.SemaphoreType.DMA((7,)),
                pltpu.SemaphoreType.DMA((matchings, n_grp)),
                pltpu.SemaphoreType.DMA((matchings, n_grp)),
            ],
            compiler_params=pltpu.CompilerParams(
                collective_id=0, has_side_effects=True, vmem_limit_bytes=62 * 2**20
            ),
        )(queries, key_rows, value_rows, order, tile_list, bias)
        return jnp.dot(attended, out_weight, preferred_element_type=jnp.float32).astype(
            jnp.bfloat16
        )

    rows_spec = P(("loop", "grp"), None)
    return jax.shard_map(
        shards,
        mesh=mesh,
        in_specs=(rows_spec, rows_spec, rows_spec, P(), rows_spec, P(None, ("loop", "grp")), P()),
        out_specs=rows_spec,
        check_vma=False,
    )
```

time: 151 us -> 79.4 us (0.53)
  the two profiles are of different devices: /device:TPU:32 before, /device:TPU:1 now
where the time goes in v1:
time: 79.4 us; the launch traced here: 79.2 us
  Pallas kernels  77.3 us (97%)
  matrix products  1.95 us (2%)
    pallas_call x1, Pallas kernels, shards(): pl.pallas_call(body, out_shape=jax.ShapeDtypeStruct((rows, width), jnp.bf...  77.3 us
    dot_general x1, matrix products, shards(): jnp.dot(attended, out_weight, preferred_element_type=jnp.float32)  1.95 us

profile of v1, /device:TPU:1, one launch (start us, length us, event | category | flops | bytes accessed | tf_op | source)
XLA Modules:
  0.0 79.2 jit_solution(12618146200746764470)
XLA Ops:
  0.0 0.0 copy-start
  0.0 77.3 %shard_map.73 = bf16[256,512]{1,0:T(8,128)(2,1)} custom-call(bf16[256,512]{1,0:T(8,128)(2,1)} %refs_0_.1, bf16[256,512]{1,0:T(8,128)(2,1)} %refs_1_.1, bf16[256,512]{1,0:T(8,128)(2,1)} %refs_2_.1, s32[3,256]{1,0:T(4,128)} %refs_3_.1, s32[1,4]{1,0:T(1,128)} %refs_4_.1, f32[3,8]{1,0:T(4,128)} %refs_5_.1), custom_call_target="tpu_custom_call" | custom-call | tf_op jit(solution)/shard_map/pallas_call | solution.py:295
  77.3 0.0 copy-done
  77.3 2.0 %convolution_convert_fusion = bf16[256,512]{1,0:T(8,128)(2,1)} fusion(bf16[256,512]{1,0:T(8,128)(2,1)} %shard_map.73, bf16[512,512]{1,0:T(8,128)(2,1)S(1)} %copy-done), kind=kOutput, calls=%fused_computation | convolution fusion | flops 134348800 | bytes 1048576 | tf_op jit(solution)/shard_map/dot_general | solution.py:325
Async XLA Ops:
  0.0 77.3 %copy-start = (bf16[512,512]{1,0:T(8,128)(2,1)S(1)}, bf16[512,512]{1,0:T(8,128)(2,1)}, u32[]{:S(2)}) copy-start(bf16[512,512]{1,0:T(8,128)(2,1)} %param.10) | copy-start | bytes 1572868

commit v2 on v1

--- a/solution.py
+++ b/solution.py
@@ -8,6 +8,7 @@
 MESH = pl.DeviceIdType.MESH
 NEG_FILL = -1e30
 RADIUS = 3
+X_RING = 4
 BUCKET_ORDER = (15, 1, 8, 2, 14, 3, 9, 4, 13, 5, 10, 6, 12, 7, 11)
 
 
@@ -62,9 +63,31 @@
     sibling = on_loop(1 - 2 * core)
     ahead, behind = on_loop(2), on_loop(-2)
     far = on_loop(6 * core - 3)
+    beyond = on_loop(10 * core - 5)
+    across = on_loop(8 * core - 4)
+    place = lax.rem(loop_pos // 2, X_RING)
+    first_core, last_core = core == 0, core == 1
+    at_first, at_last = place == 0, place == X_RING - 1
+    at_end = jnp.logical_or(
+        jnp.logical_and(at_first, first_core), jnp.logical_and(at_last, last_core)
+    )
+    past_end = jnp.logical_or(
+        jnp.logical_and(at_first, last_core), jnp.logical_and(at_last, first_core)
+    )
+    before_end = jnp.logical_or(
+        jnp.logical_and(place == 1, first_core), jnp.logical_and(place == X_RING - 2, last_core)
+    )
 
     barrier = pltpu.get_barrier_semaphore()
-    peers = [grp_peer(b) for b in BUCKET_ORDER] + [sibling, ahead, behind, far]
+    peers = [grp_peer(b) for b in BUCKET_ORDER] + [
+        sibling,
+        ahead,
+        behind,
+        far,
+        beyond,
+        on_loop(4),
+        on_loop(-4),
+    ]
     for peer in peers:
         pl.semaphore_signal(barrier, inc=1, device_id=peer, device_id_type=MESH)
 
@@ -100,35 +123,91 @@
             device_id_type=MESH,
         )
 
-    def tile_copy(src, slot, to):
+    def tile_copy(src, slot, to, send, part):
         return pltpu.make_async_remote_copy(
-            src_ref=tiles.at[src],
-            dst_ref=tiles.at[slot],
-            send_sem=tile_send.at[slot],
-            recv_sem=tile_recv.at[slot],
+            src_ref=tiles.at[src, part],
+            dst_ref=tiles.at[slot, part],
+            send_sem=tile_send.at[send, part],
+            recv_sem=tile_recv.at[slot, part],
             device_id=to,
             device_id_type=MESH,
         )
 
-    to_far = tile_copy(0, 6, far)
-    to_ahead = tile_copy(0, 2, ahead)
-    to_behind = tile_copy(0, 3, behind)
-    to_sibling = tile_copy(0, 1, sibling)
-    pass_behind = tile_copy(2, 4, sibling)
-    pass_ahead = tile_copy(3, 5, sibling)
+    def both(*args):
+        return [tile_copy(*args, part) for part in range(2)]
+
+    to_sibling = both(0, 1, sibling, 1)
+    to_ahead = both(0, 2, ahead, 2)
+    to_behind = both(0, 3, behind, 3)
+    pass_near = [None, None, both(2, 4, sibling, 4), both(3, 5, sibling, 5)]
+    to_far = both(0, 6, far, 6)
+    pass_round = [
+        None,
+        None,
+        [tile_copy(2, 3, across, 7, 1), tile_copy(2, 6, beyond, 0, 1)],
+        [tile_copy(3, 2, across, 7, 1), tile_copy(3, 6, beyond, 0, 1)],
+    ]
+    keep_ahead = jnp.logical_and(at_last, last_core)
+    keep_behind = jnp.logical_and(at_first, first_core)
+
+    def unless(flag, copies, act):
+        @pl.when(jnp.logical_not(flag))
+        def _():
+            for copy in copies:
+                act(copy)
+
+    def own_tiles(act):
+        unless(keep_ahead, to_ahead[1:], act)
+        unless(keep_behind, to_behind[1:], act)
+        act(to_ahead[0])
+        act(to_behind[0])
+        for copy in to_sibling[::-1]:
+            act(copy)
+        unless(at_end, to_far[1:], act)
+        act(to_far[0])
+
+    def passed_on(near, part, act):
+        if part == 1:
+            carries = first_core if near == 2 else last_core
+            unless(jnp.logical_not(jnp.logical_and(before_end, carries)), pass_round[near], act)
+        act(pass_near[near][part])
+
+    def begin(copy):
+        copy.start()
+
+    def sent(copy):
+        copy.wait_send()
 
     for load in loads[:3]:
         load.wait()
     gather(0)
     pl.semaphore_wait(barrier, len(peers))
-    for copy in (to_ahead, to_behind, to_far, to_sibling):
-        copy.start()
-    for b in BUCKET_ORDER:
-        exp_copy(0, b).start()
-    for j in range(1, matchings):
-        gather(j)
-        for b in BUCKET_ORDER:
-            exp_copy(j, b).start()
+    early_half = grp_pos < n_grp // 2
+
+    @pl.when(early_half)
+    def _():
+        own_tiles(begin)
+        for b in BUCKET_ORDER:
+            exp_copy(0, b).start()
+        gather(1)
+        for b in BUCKET_ORDER:
+            exp_copy(1, b).start()
+        gather(2)
+        for b in BUCKET_ORDER:
+            exp_copy(2, b).start()
+
+    @pl.when(jnp.logical_not(early_half))
+    def _():
+        for b in BUCKET_ORDER:
+            exp_copy(0, b).start()
+        gather(1)
+        own_tiles(begin)
+        for b in BUCKET_ORDER:
+            exp_copy(1, b).start()
+        gather(2)
+        for b in BUCKET_ORDER:
+            exp_copy(2, b).start()
+
 
     for load in loads[3:]:
         load.wait()
@@ -175,42 +254,6 @@
                     preferred_element_type=jnp.float32,
                 )
 
-    @pl.loop(0, 7)
-    def _(slot):
-        @pl.when(slot > 0)
-        def _():
-            tile_copy(0, slot, sibling).wait_recv()
-
-        @pl.when(slot == 2)
-        def _():
-            pass_behind.start()
-
-        @pl.when(slot == 3)
-        def _():
-            pass_ahead.start()
-
-        near = 1 - 2 * core
-        offset = jnp.where(
-            slot < 2,
-            slot * near,
-            jnp.where(
-                slot == 2,
-                -2,
-                jnp.where(
-                    slot == 3,
-                    2,
-                    jnp.where(
-                        slot == 4,
-                        -1 - 2 * core,
-                        jnp.where(slot == 5, 3 - 2 * core, 6 * core - 3),
-                    ),
-                ),
-            ),
-        )
-        absorb(slot, offset)
-
-    acc_rows[...] = jnp.transpose(run_acc[...])
-
     head_id = lax.broadcasted_iota(jnp.int32, (heads, width), 0)
     lane_id = lax.broadcasted_iota(jnp.int32, (heads, width), 1)
     in_head = jnp.logical_and(lane_id >= head_id * head, lane_id < (head_id + 1) * head)
@@ -246,8 +289,71 @@
             score = score + jnp.where(bias_row == h, bias_ref[j, h], 0.0)
         expander_e[j] = score
 
-    for j in range(matchings):
-        expander(j)
+    early = jnp.where(lax.rem(place, 2) == 0, 3, 2)
+
+    at_edge = jnp.logical_or(at_first, at_last)
+    far_soon = past_end
+    expander_step = (4, jnp.where(at_edge, 4, 6), jnp.where(at_edge, 5, 7))
+
+    @pl.loop(0, 8)
+    def _(step):
+        for j in range(matchings):
+
+            @pl.when(step == expander_step[j])
+            def _():
+                expander(j)
+
+        @pl.when(step < 7)
+        def _():
+            late = jnp.where(far_soon, jnp.where(step == 4, 6, step - 1), step)
+            late = jnp.where(jnp.logical_and(far_soon, step < 4), step, late)
+            slot = jnp.where(
+                step < 2,
+                step,
+                jnp.where(
+                    step == 2,
+                    early,
+                    jnp.where(
+                        step == 3,
+                        early + 2,
+                        jnp.where(late == 4, 5 - early, jnp.where(late == 5, 7 - early, 6)),
+                    ),
+                ),
+            )
+
+            for part in (1, 0):
+
+                @pl.when(step > 0)
+                def _():
+                    tile_copy(0, slot, sibling, 1, part).wait_recv()
+
+                for near in (2, 3):
+
+                    @pl.when(slot == near)
+                    def _():
+                        passed_on(near, part, begin)
+
+            offset = jnp.where(
+                slot < 2,
+                slot * (1 - 2 * core),
+                jnp.where(
+                    slot == 2,
+                    -2,
+                    jnp.where(
+                        slot == 3,
+                        2,
+                        jnp.where(
+                            slot == 4,
+                            -1 - 2 * core,
+                            jnp.where(slot == 5, 3 - 2 * core, 6 * core - 3),
+                        ),
+                    ),
+                ),
+            )
+            absorb(slot, offset)
+
+    acc_rows[...] = jnp.transpose(run_acc[...])
+
 
     top = run_max[...]
     for j in range(matchings):
@@ -272,8 +378,10 @@
         attended = attended + spread(weight * inverse) * partner_vals[j]
     att_ref[...] = attended.astype(jnp.bfloat16)
 
-    for copy in (to_ahead, to_behind, to_far, to_sibling, pass_behind, pass_ahead):
-        copy.wait_send()
+    own_tiles(sent)
+    for near in (2, 3):
+        for part in range(2):
+            passed_on(near, part, sent)
     for j in range(matchings):
         for b in BUCKET_ORDER:
             exp_copy(j, b).wait_send()
@@ -313,15 +421,20 @@
                 pltpu.VMEM((matchings, rows, width), jnp.float32),
                 pltpu.VMEM((matchings, heads, rows), jnp.float32),
                 pltpu.SemaphoreType.DMA((6,)),
-                pltpu.SemaphoreType.DMA((7,)),
-                pltpu.SemaphoreType.DMA((7,)),
+                pltpu.SemaphoreType.DMA((8, 2)),
+                pltpu.SemaphoreType.DMA((7, 2)),
                 pltpu.SemaphoreType.DMA((matchings, n_grp)),
                 pltpu.SemaphoreType.DMA((matchings, n_grp)),
             ],
             compiler_params=pltpu.CompilerParams(
-                collective_id=0, has_side_effects=True, vmem_limit_bytes=62 * 2**20
+                collective_id=0, has_side_effects=True, vmem_limit_bytes=40 * 2**20
             ),
-        )(queries, key_rows, value_rows, order, tile_list, bias)
+        )(
+            *(
+                pltpu.with_memory_space_constraint(x, pltpu.MemorySpace.HBM)
+                for x in (queries, key_rows, value_rows, order, tile_list, bias)
+            )
+        )
         return jnp.dot(attended, out_weight, preferred_element_type=jnp.float32).astype(
             jnp.bfloat16
         )

time: 79.4 us -> 72.2 us (0.909)
  Pallas kernels: 77.3 us -> 71 us
  matrix products: 1.95 us -> 1.01 us
    pallas_call x1, Pallas kernels: 77.3 us -> 71 us  [shards(): pl.pallas_call(body, out_shape=jax.ShapeDtypeStruct((rows, width), jnp.bf...]
    dot_general x1, matrix products: 1.95 us -> 1.01 us  [shards(): jnp.dot(attended, out_weight, preferred_element_type=jnp.float32)]
where the time goes in v2:
time: 72.2 us; the launch traced here: 72 us
  Pallas kernels  71 us (98%)
  matrix products  1.01 us (1%)
    pallas_call x1, Pallas kernels, shards(): pl.pallas_call(body, out_shape=jax.ShapeDtypeStruct((rows, width), jnp.bf...  71 us

profile of v2, /device:TPU:1, one launch (start us, length us, event | category | flops | bytes accessed | tf_op | source)
XLA Modules:
  0.0 72.0 jit_solution(7778330935535819563)
XLA Ops:
  0.0 0.0 copy-start
  0.0 71.0 %shard_map.73 = bf16[256,512]{1,0:T(8,128)(2,1)S(1)} custom-call(bf16[256,512]{1,0:T(8,128)(2,1)} %refs_0_.1, bf16[256,512]{1,0:T(8,128)(2,1)} %refs_1_.1, bf16[256,512]{1,0:T(8,128)(2,1)} %refs_2_.1, s32[3,256]{1,0:T(4,128)} %refs_3_.1, s32[1,4]{1,0:T(1,128)} %refs_4_.1, f32[3,8]{1,0:T(4,128)} %refs_5_.1), custom_call_target="tpu_custom_call" | custom-call | tf_op jit(solution)/shard_map/pallas_call | solution.py:403
  71.0 0.0 copy-done
  71.0 1.0 %convolution_convert_fusion = bf16[256,512]{1,0:T(8,128)(2,1)} fusion(bf16[256,512]{1,0:T(8,128)(2,1)S(1)} %shard_map.73, bf16[512,512]{1,0:T(8,128)(2,1)S(1)} %copy-done), kind=kOutput, calls=%fused_computation | convolution fusion | flops 134348800 | bytes 1048576 | tf_op jit(solution)/shard_map/dot_general | solution.py:438
Async XLA Ops:
  0.0 71.0 %copy-start = (bf16[512,512]{1,0:T(8,128)(2,1)S(1)}, bf16[512,512]{1,0:T(8,128)(2,1)}, u32[]{:S(2)}) copy-start(bf16[512,512]{1,0:T(8,128)(2,1)} %param.10) | copy-start | bytes 1572868

commit v3 on v2

--- a/solution.py
+++ b/solution.py
@@ -163,8 +163,12 @@
         act(to_behind[0])
         for copy in to_sibling[::-1]:
             act(copy)
+
+    def far_tile(act):
         unless(at_end, to_far[1:], act)
         act(to_far[0])
+
+    passes_end = jnp.logical_or(at_end, before_end)
 
     def passed_on(near, part, act):
         if part == 1:
@@ -187,6 +191,7 @@
     @pl.when(early_half)
     def _():
         own_tiles(begin)
+        pl.when(passes_end)(lambda: far_tile(begin))
         for b in BUCKET_ORDER:
             exp_copy(0, b).start()
         gather(1)
@@ -202,6 +207,7 @@
             exp_copy(0, b).start()
         gather(1)
         own_tiles(begin)
+        pl.when(passes_end)(lambda: far_tile(begin))
         for b in BUCKET_ORDER:
             exp_copy(1, b).start()
         gather(2)
@@ -230,29 +236,34 @@
             wanted = jnp.logical_or(wanted, tile_ref[0, t] == offset + RADIUS)
         fill = jnp.where(wanted, 0.0, NEG_FILL)
         v_turned = jnp.transpose(tiles[slot, 1].astype(jnp.float32)).astype(jnp.bfloat16)
-        for i in range(heads // 2):
-            pair = jnp.dot(
+        old, total = run_max[...], run_sum[...]
+        pairs = [
+            jnp.dot(
                 tiles[slot, 0, :, i * 2 * head : (i + 1) * 2 * head],
                 q_blocks[i],
                 preferred_element_type=jnp.float32,
             )
-            for half in range(2):
-                h = 2 * i + half
-                scores = pair[:, half * rows : (half + 1) * rows]
-                old = run_max[h : h + 1, :]
-                new = jnp.maximum(old, jnp.max(scores, axis=0, keepdims=True) + fill)
-                weights = jnp.exp(scores - (new - fill))
-                rescale = jnp.exp(old - new)
-                run_max[h : h + 1, :] = new
-                run_sum[h : h + 1, :] = run_sum[h : h + 1, :] * rescale + jnp.sum(
-                    weights, axis=0, keepdims=True
-                )
-                here = slice(h * head, (h + 1) * head)
-                run_acc[here, :] = run_acc[here, :] * rescale + jnp.dot(
-                    v_turned[here, :],
-                    weights.astype(jnp.bfloat16),
-                    preferred_element_type=jnp.float32,
-                )
+            for i in range(heads // 2)
+        ]
+        scores = [
+            pairs[h // 2][:, (h % 2) * rows : (h % 2 + 1) * rows] for h in range(heads)
+        ]
+        tops = [jnp.max(score, axis=0, keepdims=True) for score in scores]
+        new = jnp.maximum(old, jnp.concatenate(tops, axis=0) + fill)
+        shift = new - fill
+        rescale = jnp.exp(old - new)
+        sums = []
+        for h in range(heads):
+            weights = jnp.exp(scores[h] - shift[h : h + 1, :])
+            sums.append(jnp.sum(weights, axis=0, keepdims=True))
+            here = slice(h * head, (h + 1) * head)
+            run_acc[here, :] = run_acc[here, :] * rescale[h : h + 1, :] + jnp.dot(
+                v_turned[here, :],
+                weights.astype(jnp.bfloat16),
+                preferred_element_type=jnp.float32,
+            )
+        run_max[...] = new
+        run_sum[...] = total * rescale + jnp.concatenate(sums, axis=0)
 
     head_id = lax.broadcasted_iota(jnp.int32, (heads, width), 0)
     lane_id = lax.broadcasted_iota(jnp.int32, (heads, width), 1)
@@ -292,11 +303,15 @@
     early = jnp.where(lax.rem(place, 2) == 0, 3, 2)
 
     at_edge = jnp.logical_or(at_first, at_last)
-    far_soon = past_end
+    far_soon = at_edge
     expander_step = (4, jnp.where(at_edge, 4, 6), jnp.where(at_edge, 5, 7))
 
     @pl.loop(0, 8)
     def _(step):
+        @pl.when(jnp.logical_and(step == 3, jnp.logical_not(passes_end)))
+        def _():
+            far_tile(begin)
+
         for j in range(matchings):
 
             @pl.when(step == expander_step[j])
@@ -379,6 +394,7 @@
     att_ref[...] = attended.astype(jnp.bfloat16)
 
     own_tiles(sent)
+    far_tile(sent)
     for near in (2, 3):
         for part in range(2):
             passed_on(near, part, sent)

time: 72.2 us -> 71.8 us (level)
  no operation moved by 1% of the time
where the time goes in v3:
time: 71.8 us; the launch traced here: 71.7 us
  Pallas kernels  70.6 us (98%)
  matrix products  1.01 us (1%)
    pallas_call x1, Pallas kernels, shards(): pl.pallas_call(body, out_shape=jax.ShapeDtypeStruct((rows, width), jnp.bf...  70.6 us

profile of v3, /device:TPU:1, one launch (start us, length us, event | category | flops | bytes accessed | tf_op | source)
XLA Modules:
  0.0 71.7 jit_solution(15148517024733580648)
XLA Ops:
  0.0 0.0 copy-start
  0.0 70.6 %shard_map.73 = bf16[256,512]{1,0:T(8,128)(2,1)S(1)} custom-call(bf16[256,512]{1,0:T(8,128)(2,1)} %refs_0_.1, bf16[256,512]{1,0:T(8,128)(2,1)} %refs_1_.1, bf16[256,512]{1,0:T(8,128)(2,1)} %refs_2_.1, s32[3,256]{1,0:T(4,128)} %refs_3_.1, s32[1,4]{1,0:T(1,128)} %refs_4_.1, f32[3,8]{1,0:T(4,128)} %refs_5_.1), custom_call_target="tpu_custom_call" | custom-call | tf_op jit(solution)/shard_map/pallas_call | solution.py:419
  70.6 0.0 copy-done
  70.6 1.0 %convolution_convert_fusion = bf16[256,512]{1,0:T(8,128)(2,1)} fusion(bf16[256,512]{1,0:T(8,128)(2,1)S(1)} %shard_map.73, bf16[512,512]{1,0:T(8,128)(2,1)S(1)} %copy-done), kind=kOutput, calls=%fused_computation | convolution fusion | flops 134348800 | bytes 1048576 | tf_op jit(solution)/shard_map/dot_general | solution.py:454
Async XLA Ops:
  0.0 70.6 %copy-start = (bf16[512,512]{1,0:T(8,128)(2,1)S(1)}, bf16[512,512]{1,0:T(8,128)(2,1)}, u32[]{:S(2)}) copy-start(bf16[512,512]{1,0:T(8,128)(2,1)} %param.10) | copy-start | bytes 1572868

commit v4 on v3

--- a/solution.py
+++ b/solution.py
@@ -185,19 +185,22 @@
     for load in loads[:3]:
         load.wait()
     gather(0)
+    early_half = grp_pos < n_grp // 2
+
+    @pl.when(early_half)
+    def _():
+        for j in range(1, matchings):
+            gather(j)
+
     pl.semaphore_wait(barrier, len(peers))
-    early_half = grp_pos < n_grp // 2
-
     @pl.when(early_half)
     def _():
         own_tiles(begin)
         pl.when(passes_end)(lambda: far_tile(begin))
         for b in BUCKET_ORDER:
             exp_copy(0, b).start()
-        gather(1)
         for b in BUCKET_ORDER:
             exp_copy(1, b).start()
-        gather(2)
         for b in BUCKET_ORDER:
             exp_copy(2, b).start()
 

time: 71.8 us -> 71.8 us (level)
  no operation moved by 1% of the time
where the time goes in v4:
time: 71.8 us; the launch traced here: 71.7 us
  Pallas kernels  70.6 us (98%)
  matrix products  1.01 us (1%)
    pallas_call x1, Pallas kernels, shards(): pl.pallas_call(body, out_shape=jax.ShapeDtypeStruct((rows, width), jnp.bf...  70.6 us

profile of v4, /device:TPU:1, one launch (start us, length us, event | category | flops | bytes accessed | tf_op | source)
XLA Modules:
  0.0 71.7 jit_solution(13001910399965679687)
XLA Ops:
  0.0 0.0 copy-start
  0.0 70.6 %shard_map.73 = bf16[256,512]{1,0:T(8,128)(2,1)S(1)} custom-call(bf16[256,512]{1,0:T(8,128)(2,1)} %refs_0_.1, bf16[256,512]{1,0:T(8,128)(2,1)} %refs_1_.1, bf16[256,512]{1,0:T(8,128)(2,1)} %refs_2_.1, s32[3,256]{1,0:T(4,128)} %refs_3_.1, s32[1,4]{1,0:T(1,128)} %refs_4_.1, f32[3,8]{1,0:T(4,128)} %refs_5_.1), custom_call_target="tpu_custom_call" | custom-call | tf_op jit(solution)/shard_map/pallas_call | solution.py:422
  70.6 0.0 copy-done
  70.6 1.0 %convolution_convert_fusion = bf16[256,512]{1,0:T(8,128)(2,1)} fusion(bf16[256,512]{1,0:T(8,128)(2,1)S(1)} %shard_map.73, bf16[512,512]{1,0:T(8,128)(2,1)S(1)} %copy-done), kind=kOutput, calls=%fused_computation | convolution fusion | flops 134348800 | bytes 1048576 | tf_op jit(solution)/shard_map/dot_general | solution.py:457
Async XLA Ops:
  0.0 70.6 %copy-start = (bf16[512,512]{1,0:T(8,128)(2,1)S(1)}, bf16[512,512]{1,0:T(8,128)(2,1)}, u32[]{:S(2)}) copy-start(bf16[512,512]{1,0:T(8,128)(2,1)} %param.10) | copy-start | bytes 1572868
